TPU v7x, 256 devices: a whole 4x4x8 slice. The times are simulated.
256 devices in a mesh: ctx: 64 (over y, z, core), head: 4 (over x).
Axes of the slice: x: 4, y: 4, z: 8, core: 2. Of those that a mesh axis runs over, the one named last changes fastest.
Arguments:
- query: bfloat16 [64, 2, 512, 4096], P('ctx', None, None, 'head'), may hold values from -48 to 48
- key: bfloat16 [64, 2, 512, 512], P('ctx', None, 'head'), may hold values from -18 to 18
- value: bfloat16 [64, 2, 512, 512], P('ctx', None, 'head'), may hold values from -6 to 6
- d_out: bfloat16 [64, 2, 512, 4096], P('ctx', None, None, 'head'), may hold values from -6 to 6
- doc_start: int32 [512], replicated, may hold values from 0 to 1, as said below
Outputs:
- d_query: bfloat16 [64, 2, 512, 4096], P('ctx', None, None, 'head')
- d_key: bfloat16 [64, 2, 512, 512], P('ctx', None, 'head')
- d_value: bfloat16 [64, 2, 512, 512], P('ctx', None, 'head')
Inputs may be any that keep to these rules, and one draw needn't show every extreme that they name: `doc_start`: 1 where a document begins at that block of 128 tokens (blocks in sequence order); block 0 begins one; from every beginning the next beginning, or the end of the sequence, is 1 to 3 blocks away; the first block of every span after the first lies inside a document of exactly 3 blocks that began in the span before.
All inputs are finite; a program needn't handle non-finite values.
Results may differ from a plain program's by a relative error of at most 0.039.
Values may be sent and summed in bfloat16 or wider, within the bound.
A program may use at most 64 MiB of HBM per device.

v0:
```python
import jax
import jax.numpy as jnp
from jax import lax
from jax.sharding import PartitionSpec as P

HD = 128
BLK = 128
GROUP = 8


def padded_2(cells, sides, width):
    for axis, dim in sides:
        count = lax.axis_size(axis)
        ends = count - 1
        head = lax.slice_in_dim(cells, 0, width, axis=dim)
        tail = lax.slice_in_dim(cells, cells.shape[dim] - width, cells.shape[dim], axis=dim)
        cells = jnp.concatenate(
            [
                lax.ppermute(tail, axis, [(i, (i + 1) % count) for i in range(ends)]),
                cells,
                lax.ppermute(head, axis, [((i + 1) % count, i) for i in range(ends)]),
            ],
            axis=dim,
        )
    return cells


def windowed(extended, reach_rows, blocks):
    pieces = []
    for offset in range(reach_rows // BLK + 1):
        sliced = lax.slice_in_dim(extended, offset * BLK, offset * BLK + blocks * BLK, axis=0)
        pieces.append(sliced.reshape((blocks, BLK) + extended.shape[1:]))
    return jnp.concatenate(pieces, axis=1)


def unwindowed(windows, reach_rows, blocks):
    summed = None
    for offset in range(reach_rows // BLK + 1):
        sliced = windows[:, offset * BLK : (offset + 1) * BLK].reshape(
            (blocks * BLK,) + windows.shape[2:]
        )
        padded = jnp.pad(
            sliced, ((offset * BLK, reach_rows - offset * BLK),) + ((0, 0),) * (windows.ndim - 2)
        )
        summed = padded if summed is None else summed + padded
    return summed


def span_grads(queries, grads_out, keys_ext, values_ext, doc_begins, span_start, reach_rows):
    blocks = queries.shape[0] // BLK
    kv_heads = keys_ext.shape[1] // HD
    score_scale = HD ** (-0.5)
    q_blocks = queries.reshape(blocks, BLK, kv_heads, GROUP, HD)
    do_blocks = grads_out.reshape(blocks, BLK, kv_heads, GROUP, HD)
    k_windows = windowed(keys_ext.reshape(-1, kv_heads, HD), reach_rows, blocks)
    v_windows = windowed(values_ext.reshape(-1, kv_heads, HD), reach_rows, blocks)
    row_pos = jnp.arange(BLK, dtype=jnp.int32)[None, :, None]
    col_pos = jnp.arange(reach_rows + BLK, dtype=jnp.int32)[None, None, :]
    key_pos = (
        span_start - reach_rows + jnp.arange(blocks, dtype=jnp.int32)[:, None, None] * BLK + col_pos
    )
    visible = (col_pos <= row_pos + reach_rows) & (key_pos >= doc_begins[:, None, None])
    visible = visible[:, None, None]
    scores = (
        jnp.einsum("btgjd,bkgd->bgjtk", q_blocks, k_windows, preferred_element_type=jnp.float32)
        * score_scale
    )
    peak = jnp.max(jnp.where(visible, scores, -1e30), axis=-1, keepdims=True)
    weights = jnp.exp(jnp.where(visible, scores - peak, -1e30))
    probs = weights / jnp.sum(weights, axis=-1, keepdims=True)
    probs_b = probs.astype(jnp.bfloat16)
    outputs = jnp.einsum(
        "bgjtk,bkgd->btgjd", probs_b, v_windows, preferred_element_type=jnp.float32
    ).astype(jnp.bfloat16)
    deltas = jnp.sum(do_blocks.astype(jnp.float32) * outputs.astype(jnp.float32), axis=-1)
    dprobs = jnp.einsum(
        "btgjd,bkgd->bgjtk", do_blocks, v_windows, preferred_element_type=jnp.float32
    )
    dscores = (
        probs * (dprobs - jnp.transpose(deltas, (0, 2, 3, 1))[..., None]) * score_scale
    ).astype(jnp.bfloat16)
    d_queries = jnp.einsum(
        "bgjtk,bkgd->btgjd", dscores, k_windows, preferred_element_type=jnp.float32
    ).astype(jnp.bfloat16)
    dk_windows = jnp.einsum(
        "bgjtk,btgjd->bkgd", dscores, q_blocks, preferred_element_type=jnp.float32
    )
    dv_windows = jnp.einsum(
        "bgjtk,btgjd->bkgd", probs_b, do_blocks, preferred_element_type=jnp.float32
    )
    return (
        d_queries.reshape(blocks * BLK, -1),
        unwindowed(dk_windows, reach_rows, blocks).reshape(-1, kv_heads * HD),
        unwindowed(dv_windows, reach_rows, blocks).reshape(-1, kv_heads * HD),
    )


def per_device(query, key, value, d_out, doc_start):
    kv_key, kv_value = (
        lax.all_to_all(key, "head", split_axis=3, concat_axis=2, tiled=True),
        lax.all_to_all(value, "head", split_axis=3, concat_axis=2, tiled=True),
    )
    span_rows = kv_key.shape[2]
    ctx_index = lax.axis_index("ctx")
    ctx_count = lax.axis_size("ctx")
    is_last = ctx_index == ctx_count - 1
    rim_from = span_rows - span_rows
    outgoing = jnp.stack(
        [
            jnp.stack([kv_key[0, 1, rim_from:], kv_value[0, 1, rim_from:]]),
            jnp.stack([kv_key[0, 0, rim_from:], kv_value[0, 0, rim_from:]]),
        ]
    )
    incoming = padded_2(outgoing, (("ctx", 0),), 1)
    previous = [incoming[0], jnp.where(is_last, outgoing[1], incoming[3])]
    run_begin = (
        lax.cummax(
            jnp.where(doc_start == 1, jnp.arange(doc_start.shape[0], dtype=jnp.int32), 0), axis=0
        )
        * BLK
    )
    blocks = span_rows // BLK
    span_results = []
    for span_slot in range(2):
        span_id = ctx_index if span_slot == 0 else 2 * ctx_count - 1 - ctx_index
        span_start = span_id * span_rows
        doc_begins = lax.dynamic_slice_in_dim(run_begin, span_id * blocks, blocks)
        keys_ext = jnp.concatenate([previous[span_slot][0], kv_key[0, span_slot]], axis=0)
        values_ext = jnp.concatenate([previous[span_slot][1], kv_value[0, span_slot]], axis=0)
        span_results.append(
            span_grads(
                query[0, span_slot],
                d_out[0, span_slot],
                keys_ext,
                values_ext,
                doc_begins,
                span_start,
                span_rows,
            )
        )
    partials = jnp.stack(
        [
            jnp.stack([span_results[0][1][:span_rows], span_results[0][2][:span_rows]]),
            jnp.stack([span_results[1][1][:span_rows], span_results[1][2][:span_rows]]),
        ]
    )
    returned = padded_2(partials.astype(jnp.bfloat16), (("ctx", 0),), 1).astype(partials.dtype)
    added_parts = [returned[3] + jnp.where(is_last, partials[1], 0.0), returned[0]]
    key_grads = []
    value_grads = []
    for span_slot in range(2):
        own_key = (
            span_results[span_slot][1][span_rows:].at[rim_from:].add(added_parts[span_slot][0])
        )
        own_value = (
            span_results[span_slot][2][span_rows:].at[rim_from:].add(added_parts[span_slot][1])
        )
        key_grads.append(own_key.astype(jnp.bfloat16))
        value_grads.append(own_value.astype(jnp.bfloat16))
    d_query = jnp.stack([span_results[0][0], span_results[1][0]])[None]
    key_layout = jnp.stack(key_grads)[None]
    value_layout = jnp.stack(value_grads)[None]
    d_key, d_value = (
        lax.all_to_all(key_layout, "head", split_axis=2, concat_axis=3, tiled=True),
        lax.all_to_all(value_layout, "head", split_axis=2, concat_axis=3, tiled=True),
    )
    return (d_query, d_key, d_value)


def solution(mesh):
    return jax.shard_map(
        per_device,
        mesh=mesh,
        in_specs=(
            P("ctx", None, None, "head"),
            P("ctx", None, "head", None),
            P("ctx", None, "head", None),
            P("ctx", None, None, "head"),
            P(),
        ),
        out_specs=(
            P("ctx", None, None, "head"),
            P("ctx", None, "head", None),
            P("ctx", None, "head", None),
        ),
        check_vma=False,
    )
```

profile of v0, /device:TPU:26, one launch (start us, length us, event | category | flops | bytes accessed | tf_op | source)
XLA Modules:
  0.0 143.1 jit_solution(6247647339542804097)
XLA Ops:
  0.6 1.8 %copy.44 = bf16[1,2,128,512]{2,1,0,3:T(2,128)(2,1)} copy(bf16[1,2,128,512]{3,2,1,0:T(8,128)(2,1)} %param.22) | data formatting | bytes 524288 | tf_op args[1]
  2.5 4.8 %all-to-all-start = ((bf16[1,2,128,512]{2,1,0,3:T(2,128)(2,1)}), bf16[1,2,128,512]{2,1,0,3:T(2,128)(2,1)S(1)}, u32[]{:S(2)}, u32[]{:S(2)}) async-start(bf16[1,2,128,512]{2,1,0,3:T(2,128)(2,1)} %copy.44), calls=%async_computation | async-start | bytes 524288 | tf_op jit(solution)/shard_map/all_to_all | solution.py:100
  8.6 1.8 %copy.46 = bf16[1,2,128,512]{2,1,0,3:T(2,128)(2,1)} copy(bf16[1,2,128,512]{3,2,1,0:T(8,128)(2,1)} %param.23) | data formatting | bytes 524288 | tf_op args[2]
  12.1 4.6 %slice_bitcast_fusion.3 = (bf16[64,8,8,128]{3,1,2,0:T(8,128)(2,1)}, f32[64,8,8,128]{3,1,2,0:T(8,128)}, f32[64,8,8,128]{3,1,2,0:T(8,128)}, bf16[64,8,8,128]{3,1,2,0:T(8,128)(2,1)}) fusion(bf16[1,2,512,1024]{3,2,1,0:T(8,128)(2,1)} %param.24), kind=kLoop, calls=%fused_computation.68 | loop fusion | flops 1048576 | bytes 8388608
  16.9 4.8 %all-to-all-start.1 = ((bf16[1,2,128,512]{2,1,0,3:T(2,128)(2,1)}), bf16[1,2,128,512]{2,1,0,3:T(2,128)(2,1)S(1)}, u32[]{:S(2)}, u32[]{:S(2)}) async-start(bf16[1,2,128,512]{2,1,0,3:T(2,128)(2,1)} %copy.46), calls=%async_computation.1 | async-start | bytes 524288 | tf_op jit(solution)/shard_map/all_to_all | solution.py:101
  22.5 4.3 %all-to-all-done.1 = bf16[1,2,128,512]{2,1,0,3:T(2,128)(2,1)S(1)} async-done(((bf16[1,2,128,512]{2,1,0,3:T(2,128)(2,1)}), bf16[1,2,128,512]{2,1,0,3:T(2,128)(2,1)S(1)}, u32[]{:S(2)}, u32[]{:S(2)}) %all-to-all-start.1) | async-done | bytes 262176 | tf_op jit(solution)/shard_map/all_to_all | solution.py:101
  28.8 5.4 %collective-permute-start.1 = (bf16[1,2,512,128]{3,2,1,0:T(8,128)(2,1)}, bf16[1,2,512,128]{3,2,1,0:T(8,128)(2,1)}, u32[]{:S(2)}, u32[]{:S(2)}) collective-permute-start(bf16[1,2,512,128]{3,2,1,0:T(8,128)(2,1)} %maximum_bitcast_fusion.1), channel_id=1, source_target_pairs={{4,0},{8,4},{12,8},{16,12},{20,16},{24,20},{28,24},{32,28},{36,32}... | collective-permute-start | bytes 786440 | tf_op jit(solution)/shard_map/ppermute | solution.py:21
  34.8 2.5 %copy.98 = bf16[64,8,8,128]{3,2,1,0:T(8,128)(2,1)} copy(bf16[64,8,8,128]{3,1,2,0:T(8,128)(2,1)} %get-tuple-element.83) | data formatting | bytes 2097152
  38.8 3.4 %copy.99 = f32[64,8,8,128]{3,2,1,0:T(8,128)} copy(f32[64,8,8,128]{3,1,2,0:T(8,128)} %get-tuple-element.84) | data formatting | bytes 4194304
  42.2 2.9 %copy.52 = f32[4,128,1,8,128]{1,4,3,0,2:T(8,128)} copy(f32[4,128,1,8,128]{4,3,2,1,0:T(8,128)} %bitcast.414) | data formatting | bytes 4194304 | tf_op jit(solution)/shard_map/convert_element_type | solution.py:75
  45.1 3.4 %copy.102 = f32[64,8,8,128]{3,2,1,0:T(8,128)} copy(f32[64,8,8,128]{3,1,2,0:T(8,128)} %get-tuple-element.85) | data formatting | bytes 4194304
  48.5 2.9 %copy.60 = f32[4,128,1,8,128]{1,4,3,0,2:T(8,128)} copy(f32[4,128,1,8,128]{4,3,2,1,0:T(8,128)} %bitcast.415) | data formatting | bytes 4194304 | tf_op jit(solution)/shard_map/convert_element_type | solution.py:75
  51.4 2.2 %broadcast_and_fusion.1 = (pred[4,128,640]{1,2,0:T(8,128)(4,1)S(1)}, pred[4,128,640]{1,2,0:T(8,128)(4,1)S(1)}) fusion(pred[4,640]{1,0:T(4,128)(4,1)S(1)} %get-tuple-element.162, pred[128,640]{0,1:T(8,128)(4,1)} %iota_compare_fusion, pred[4,640]{1,0:T(4,128)(4,1)S(1)} %get-tuple-element.161), kind=kLoop, calls=%fused_computation.78 | loop fusion | flops 655360 | bytes 742400 | tf_op jit(solution)/shard_map/and | solution.py:62
  53.6 1.8 %fusion.81 = (bf16[1,2,512,128]{3,2,1,0:T(8,128)(2,1)}, bf16[2,512,128]{2,1,0:T(8,128)(2,1)S(1)}) fusion(bf16[1,512,128]{2,1,0:T(8,128)(2,1)} %get-tuple-element.159, bf16[1,512,128]{2,1,0:T(8,128)(2,1)} %get-tuple-element.114, bf16[1,2,512,128]{3,2,1,0:T(8,128)(2,1)} %collective-permute-done.1, pred[]{:T(512)S(6)} %eq.11), kind=kLoop, calls=%fused_computation.125 | loop fusion | flops 262144 | bytes 1048577 | tf_op jit(solution)/shard_map/stack | solution.py:108
  55.4 2.1 %collective-permute-start = (bf16[1,2,512,128]{3,2,1,0:T(8,128)(2,1)}, bf16[1,2,512,128]{3,2,1,0:T(8,128)(2,1)}, u32[]{:S(2)}, u32[]{:S(2)}) collective-permute-start(bf16[1,2,512,128]{3,2,1,0:T(8,128)(2,1)} %get-tuple-element.135), channel_id=1, source_target_pairs={{0,4},{4,8},{8,12},{12,16},{16,20},{20,24},{24,28},{28,32},{32,36}... | collective-permute-start | bytes 786440 | tf_op jit(solution)/shard_map/ppermute | solution.py:19
  60.5 2.4 %fusion.15 = f32[4,8,128]{2,1,0:T(8,128)S(1)} fusion(f32[4,640,128,8]{2,1,3,0:T(8,128)S(1)} %get-tuple-element.152, f32[4,8,128]{2,1,0:T(8,128)S(1)} %get-tuple-element.151, pred[4,128,640]{1,2,0:T(8,128)(4,1)S(1)} %get-tuple-element.148), kind=kLoop, calls=%fused_computation.21 | loop fusion | flops 10481664 | bytes 10846208 | tf_op jit(solution)/shard_map/reduce_sum | solution.py:70
  62.9 3.1 %fusion.41 = f32[4,640,1,128]{3,1,0,2:T(8,128)S(1)} fusion(bf16[4,128,8,128]{3,2,1,0:T(8,128)(2,1)S(1)} %bitcast.439, f32[4,8,128]{2,1,0:T(8,128)S(1)} %fusion.15, f32[4,8,128]{2,1,0:T(8,128)S(1)} %get-tuple-element.151, f32[4,640,128,8]{2,1,3,0:T(8,128)S(1)} %get-tuple-element.152, pred[4,128,640]{1,2,0:T(8,128)(4,1)S(1)} %get-tuple-element.148), kind=kOutput, calls=%fused_computation.50 | convolution fusion | flops 684195840 | bytes 13205504 | tf_op jit(solution)/shard_map/bgjtk,btgjd->bkgd/dot_general | solution.py:88
  66.1 3.2 %fusion.29 = f32[4,128,8]{1,2,0:T(8,128)S(1)} fusion(f32[4,128,1,8,128]{1,4,3,0,2:T(8,128)S(1)} %copy-done.6, bf16[4,640,1,128]{3,1,0,2:T(8,128)(2,1)S(1)} %constant_dynamic-update-slice_fusion.15, f32[4,8,128]{2,1,0:T(8,128)S(1)} %fusion.15, f32[4,8,128]{2,1,0:T(8,128)S(1)} %get-tuple-element.151, f32[4,640,128,8]{2,1,3,0:T(8,128)S(1)} %get-tuple-element.152, ...), kind=kOutput, calls=%fused_computation.37 | convolution fusion | flops 686288896 | bytes 13615104 | tf_op jit(solution)/shard_map/bgjtk,bkgd->btgjd/dot_general | solution.py:72
  69.2 4.2 %fusion.17 = bf16[4,8,128,640]{2,3,1,0:T(8,128)(2,1)S(1)} fusion(f32[4,8,128]{2,1,0:T(8,128)S(1)} %bitcast.468, f32[4,8,128]{2,1,0:T(8,128)S(1)} %fusion.15, f32[4,8,128]{2,1,0:T(8,128)S(1)} %get-tuple-element.151, f32[4,640,128,8]{2,1,3,0:T(8,128)S(1)} %get-tuple-element.152, pred[4,128,640]{1,2,0:T(8,128)(4,1)S(1)} %get-tuple-element.148, ...), kind=kOutput, calls=%fused_computation.23 | convolution fusion | flops 692060160 | bytes 17809408 | tf_op jit(solution)/shard_map/btgjd,bkgd->bgjtk/dot_general | solution.py:76
  76.2 2.1 %collective-permute-start.2 = (bf16[1,2,512,128]{3,2,1,0:T(8,128)(2,1)S(1)}, bf16[1,2,512,128]{3,2,1,0:T(8,128)(2,1)S(1)}, u32[]{:S(2)}, u32[]{:S(2)}) collective-permute-start(bf16[1,2,512,128]{3,2,1,0:T(8,128)(2,1)S(1)} %fusion.76), channel_id=1, source_target_pairs={{0,4},{4,8},{8,12},{12,16},{16,20},{20,24},{24,28},{28,32},{32,36}... | collective-permute-start | bytes 786440 | tf_op jit(solution)/shard_map/ppermute | solution.py:19
  81.5 2.4 %fusion.13 = f32[4,8,128]{2,1,0:T(8,128)S(1)} fusion(f32[4,640,128,8]{2,1,3,0:T(8,128)S(1)} %get-tuple-element.154, f32[4,8,128]{2,1,0:T(8,128)S(1)} %get-tuple-element.153, pred[4,128,640]{1,2,0:T(8,128)(4,1)S(1)} %get-tuple-element.147), kind=kLoop, calls=%fused_computation.19 | loop fusion | flops 10481664 | bytes 10846208 | tf_op jit(solution)/shard_map/reduce_sum | solution.py:70
  83.9 4.2 %fusion.38 = f32[4,640,1,128]{3,1,0,2:T(8,128)S(1)} fusion(bf16[4,128,8,128]{3,2,1,0:T(8,128)(2,1)} %bitcast.437, f32[4,8,128]{2,1,0:T(8,128)S(1)} %fusion.13, f32[4,8,128]{2,1,0:T(8,128)S(1)} %get-tuple-element.153, f32[4,640,128,8]{2,1,3,0:T(8,128)S(1)} %get-tuple-element.154, pred[4,128,640]{1,2,0:T(8,128)(4,1)S(1)} %get-tuple-element.147), kind=kOutput, calls=%fused_computation.49 | convolution fusion | flops 684195840 | bytes 13205504 | tf_op jit(solution)/shard_map/bgjtk,btgjd->bkgd/dot_general | solution.py:88
  88.2 4.4 %fusion.31 = f32[4,128,8]{1,2,0:T(8,128)S(1)} fusion(f32[4,128,1,8,128]{1,4,3,0,2:T(8,128)S(1)} %copy-done.5, bf16[4,640,1,128]{3,1,0,2:T(8,128)(2,1)} %copy-done.14, f32[4,8,128]{2,1,0:T(8,128)S(1)} %fusion.13, f32[4,8,128]{2,1,0:T(8,128)S(1)} %get-tuple-element.153, f32[4,640,128,8]{2,1,3,0:T(8,128)S(1)} %get-tuple-element.154, ...), kind=kOutput, calls=%fused_computation.40 | convolution fusion | flops 686288896 | bytes 13615104 | tf_op jit(solution)/shard_map/bgjtk,bkgd->btgjd/dot_general | solution.py:72
  92.6 4.2 %fusion.16 = bf16[4,8,128,640]{2,3,1,0:T(8,128)(2,1)S(1)} fusion(f32[4,8,128]{2,1,0:T(8,128)S(1)} %bitcast.469, f32[4,8,128]{2,1,0:T(8,128)S(1)} %fusion.13, f32[4,8,128]{2,1,0:T(8,128)S(1)} %get-tuple-element.153, f32[4,640,128,8]{2,1,3,0:T(8,128)S(1)} %get-tuple-element.154, pred[4,128,640]{1,2,0:T(8,128)(4,1)S(1)} %get-tuple-element.147, ...), kind=kOutput, calls=%fused_computation.22 | convolution fusion | flops 692060160 | bytes 17809408 | tf_op jit(solution)/shard_map/btgjd,bkgd->bgjtk/dot_general | solution.py:76
  97.0 2.1 %copy-done = bf16[4,8,128,640]{2,3,1,0:T(8,128)(2,1)} copy-done((bf16[4,8,128,640]{2,3,1,0:T(8,128)(2,1)}, bf16[4,8,128,640]{2,3,1,0:T(8,128)(2,1)S(1)}, u32[]{:S(2)}) %copy-start) | copy-done | bytes 5242904
  101.7 6.0 %collective-permute-start.3 = (bf16[1,2,512,128]{3,2,1,0:T(8,128)(2,1)S(1)}, bf16[1,2,512,128]{3,2,1,0:T(8,128)(2,1)S(1)}, u32[]{:S(2)}, u32[]{:S(2)}) collective-permute-start(bf16[1,2,512,128]{3,2,1,0:T(8,128)(2,1)S(1)} %maximum_bitcast_fusion.2), channel_id=1, source_target_pairs={{4,0},{8,4},{12,8},{16,12},{20,16},{24,20},{28,24},{32,28},{36,32}... | collective-permute-start | bytes 786440 | tf_op jit(solution)/shard_map/ppermute | solution.py:21
  107.7 2.0 %fusion.45 = bf16[4,128,1,8,128]{1,4,3,0,2:T(8,128)(2,1)} fusion(bf16[4,8,128,640]{2,3,1,0:T(8,128)(2,1)S(1)} %fusion.17, bf16[4,640,1,128]{3,1,0,2:T(8,128)(2,1)S(1)} %constant_dynamic-update-slice_fusion.10), kind=kOutput, calls=%fused_computation.52 | convolution fusion | flops 671612928 | bytes 6946816 | tf_op jit(solution)/shard_map/bgjtk,bkgd->btgjd/dot_general | solution.py:82
  115.9 4.8 %all-to-all-start.3 = ((bf16[1,2,512,128]{3,1,0,2:T(2,128)(2,1)}), bf16[1,2,512,128]{3,1,0,2:T(2,128)(2,1)S(1)}, u32[]{:S(2)}, u32[]{:S(2)}) async-start(bf16[1,2,512,128]{3,1,0,2:T(2,128)(2,1)} %copy.71), calls=%async_computation.3 | async-start | bytes 524288 | tf_op jit(solution)/shard_map/all_to_all | solution.py:165
  123.5 2.5 %all-to-all-done.3 = bf16[1,2,512,128]{3,1,0,2:T(2,128)(2,1)S(1)} async-done(((bf16[1,2,512,128]{3,1,0,2:T(2,128)(2,1)}), bf16[1,2,512,128]{3,1,0,2:T(2,128)(2,1)S(1)}, u32[]{:S(2)}, u32[]{:S(2)}) %all-to-all-start.3) | async-done | bytes 262176 | tf_op jit(solution)/shard_map/all_to_all | solution.py:165
  126.0 4.8 %all-to-all-start.2 = ((bf16[1,2,512,128]{3,1,0,2:T(2,128)(2,1)}), bf16[1,2,512,128]{3,1,0,2:T(2,128)(2,1)S(1)}, u32[]{:S(2)}, u32[]{:S(2)}) async-start(bf16[1,2,512,128]{3,1,0,2:T(2,128)(2,1)} %maximum_bitcast_fusion.3), calls=%async_computation.2 | async-start | bytes 524288 | tf_op jit(solution)/shard_map/all_to_all | solution.py:164
  130.8 4.5 %fusion.44 = bf16[4,128,1,8,128]{1,4,3,0,2:T(8,128)(2,1)} fusion(bf16[4,8,128,640]{2,3,1,0:T(8,128)(2,1)} %copy-done, bf16[4,640,1,128]{3,1,0,2:T(8,128)(2,1)S(1)} %constant_dynamic-update-slice_fusion), kind=kOutput, calls=%fused_computation.51 | convolution fusion | flops 671612928 | bytes 6946816 | tf_op jit(solution)/shard_map/bgjtk,bkgd->btgjd/dot_general | solution.py:82
  138.3 2.7 %maximum_bitcast_fusion = bf16[1,2,512,1024]{3,2,1,0:T(8,128)(2,1)} fusion(bf16[1,512,1024]{2,1,0:T(8,128)(2,1)S(1)} %copy-done.1, bf16[1,512,1024]{2,1,0:T(8,128)(2,1)} %stack_reshape.6), kind=kLoop, calls=%fused_computation.34 | loop fusion | flops 1048576 | bytes 4194304 | tf_op jit(solution)/shard_map/broadcast_in_dim | solution.py:160
  (118 shorter events, 33.2 us)
Async XLA Ops:
  2.5 14.4 %all-to-all-start = ((bf16[1,2,128,512]{2,1,0,3:T(2,128)(2,1)}), bf16[1,2,128,512]{2,1,0,3:T(2,128)(2,1)S(1)}, u32[]{:S(2)}, u32[]{:S(2)}) async-start(bf16[1,2,128,512]{2,1,0,3:T(2,128)(2,1)} %copy.44), calls=%async_computation | async-start | bytes 524288 | tf_op jit(solution)/shard_map/all_to_all | solution.py:100
  16.9 10.0 %all-to-all-start.1 = ((bf16[1,2,128,512]{2,1,0,3:T(2,128)(2,1)}), bf16[1,2,128,512]{2,1,0,3:T(2,128)(2,1)S(1)}, u32[]{:S(2)}, u32[]{:S(2)}) async-start(bf16[1,2,128,512]{2,1,0,3:T(2,128)(2,1)} %copy.46), calls=%async_computation.1 | async-start | bytes 524288 | tf_op jit(solution)/shard_map/all_to_all | solution.py:101
  28.8 24.8 %collective-permute-start.1 = (bf16[1,2,512,128]{3,2,1,0:T(8,128)(2,1)}, bf16[1,2,512,128]{3,2,1,0:T(8,128)(2,1)}, u32[]{:S(2)}, u32[]{:S(2)}) collective-permute-start(bf16[1,2,512,128]{3,2,1,0:T(8,128)(2,1)} %maximum_bitcast_fusion.1), channel_id=1, source_target_pairs={{4,0},{8,4},{12,8},{16,12},{20,16},{24,20},{28,24},{32,28},{36,32}... | collective-permute-start | bytes 786440 | tf_op jit(solution)/shard_map/ppermute | solution.py:21
  55.4 23.0 %collective-permute-start = (bf16[1,2,512,128]{3,2,1,0:T(8,128)(2,1)}, bf16[1,2,512,128]{3,2,1,0:T(8,128)(2,1)}, u32[]{:S(2)}, u32[]{:S(2)}) collective-permute-start(bf16[1,2,512,128]{3,2,1,0:T(8,128)(2,1)} %get-tuple-element.135), channel_id=1, source_target_pairs={{0,4},{4,8},{8,12},{12,16},{16,20},{20,24},{24,28},{28,32},{32,36}... | collective-permute-start | bytes 786440 | tf_op jit(solution)/shard_map/ppermute | solution.py:19
  62.9 3.1 %copy-start.6 = (f32[4,128,1,8,128]{1,4,3,0,2:T(8,128)S(1)}, f32[4,128,1,8,128]{1,4,3,0,2:T(8,128)}, u32[]{:S(2)}) copy-start(f32[4,128,1,8,128]{1,4,3,0,2:T(8,128)} %copy.60) | copy-start | bytes 6291460
  73.5 6.0 %copy-start.11 = (bf16[512,128]{1,0:T(8,128)(2,1)S(1)}, bf16[512,128]{1,0:T(8,128)(2,1)}, u32[]{:S(2)}) copy-start(bf16[512,128]{1,0:T(8,128)(2,1)} %get-tuple-element.115) | copy-start | bytes 393220
  73.5 6.1 %copy-start.10 = (bf16[512,128]{1,0:T(8,128)(2,1)S(1)}, bf16[512,128]{1,0:T(8,128)(2,1)}, u32[]{:S(2)}) copy-start(bf16[512,128]{1,0:T(8,128)(2,1)} %get-tuple-element.158) | copy-start | bytes 393220
  73.6 6.1 %copy-start.13 = (bf16[1,1,512,128]{3,2,1,0:T(8,128)(2,1)S(1)}, bf16[1,1,512,128]{3,2,1,0:T(8,128)(2,1)}, u32[]{:S(2)}) copy-start(bf16[1,1,512,128]{3,2,1,0:T(8,128)(2,1)} %get-tuple-element.160) | copy-start | bytes 393220
  73.6 6.2 %copy-start.12 = (bf16[1,1,512,128]{3,2,1,0:T(8,128)(2,1)S(1)}, bf16[1,1,512,128]{3,2,1,0:T(8,128)(2,1)}, u32[]{:S(2)}) copy-start(bf16[1,1,512,128]{3,2,1,0:T(8,128)(2,1)} %get-tuple-element.113) | copy-start | bytes 393220
  76.1 5.4 %copy-start.2 = (f32[1,512,128]{2,1,0:T(8,128)}, f32[1,512,128]{2,1,0:T(8,128)S(1)}, u32[]{:S(2)}) copy-start(f32[1,512,128]{2,1,0:T(8,128)S(1)} %get-tuple-element.111) | copy-start | bytes 786436
  76.2 5.4 %copy-start.4 = (f32[1024,1,128]{2,0,1:T(8,128)}, f32[1024,1,128]{2,0,1:T(8,128)S(1)}, u32[]{:S(2)}) copy-start(f32[1024,1,128]{2,0,1:T(8,128)S(1)} %pad_add_fusion.1) | copy-start | bytes 1572868
  76.2 36.5 %collective-permute-start.2 = (bf16[1,2,512,128]{3,2,1,0:T(8,128)(2,1)S(1)}, bf16[1,2,512,128]{3,2,1,0:T(8,128)(2,1)S(1)}, u32[]{:S(2)}, u32[]{:S(2)}) collective-permute-start(bf16[1,2,512,128]{3,2,1,0:T(8,128)(2,1)S(1)} %fusion.76), channel_id=1, source_target_pairs={{0,4},{4,8},{8,12},{12,16},{16,20},{20,24},{24,28},{28,32},{32,36}... | collective-permute-start | bytes 786440 | tf_op jit(solution)/shard_map/ppermute | solution.py:19
  79.7 4.2 %copy-start.14 = (bf16[4,640,1,128]{3,1,0,2:T(8,128)(2,1)}, bf16[4,640,1,128]{3,1,0,2:T(8,128)(2,1)S(1)}, u32[]{:S(2)}) copy-start(bf16[4,640,1,128]{3,1,0,2:T(8,128)(2,1)S(1)} %constant_dynamic-update-slice_fusion.5) | copy-start | bytes 1966084
  83.9 4.2 %copy-start.5 = (f32[4,128,1,8,128]{1,4,3,0,2:T(8,128)S(1)}, f32[4,128,1,8,128]{1,4,3,0,2:T(8,128)}, u32[]{:S(2)}) copy-start(f32[4,128,1,8,128]{1,4,3,0,2:T(8,128)} %copy.52) | copy-start | bytes 6291460
  88.2 4.4 %copy-start.9 = (bf16[64,8,8,128]{3,2,1,0:T(8,128)(2,1)S(1)}, bf16[64,8,8,128]{3,2,1,0:T(8,128)(2,1)}, u32[]{:S(2)}) copy-start(bf16[64,8,8,128]{3,2,1,0:T(8,128)(2,1)} %copy.98) | copy-start | bytes 3145732
  88.2 4.4 %copy-start.15 = (bf16[4,640,1,128]{3,1,0,2:T(8,128)(2,1)S(1)}, bf16[4,640,1,128]{3,1,0,2:T(8,128)(2,1)}, u32[]{:S(2)}) copy-start(bf16[4,640,1,128]{3,1,0,2:T(8,128)(2,1)} %copy-done.14) | copy-start | bytes 1966084
  96.8 2.3 %copy-start = (bf16[4,8,128,640]{2,3,1,0:T(8,128)(2,1)}, bf16[4,8,128,640]{2,3,1,0:T(8,128)(2,1)S(1)}, u32[]{:S(2)}) copy-start(bf16[4,8,128,640]{2,3,1,0:T(8,128)(2,1)S(1)} %fusion.16) | copy-start | bytes 15728644
  97.0 10.7 %copy-start.7 = (f32[1024,1,128]{2,0,1:T(8,128)}, f32[1024,1,128]{2,0,1:T(8,128)S(1)}, u32[]{:S(2)}) copy-start(f32[1024,1,128]{2,0,1:T(8,128)S(1)} %pad_add_fusion) | copy-start | bytes 1572868
  100.7 12.0 %copy-start.3 = (f32[1,512,128]{2,1,0:T(8,128)S(1)}, f32[1,512,128]{2,1,0:T(8,128)}, u32[]{:S(2)}) copy-start(f32[1,512,128]{2,1,0:T(8,128)} %copy-done.2) | copy-start | bytes 786436
  100.9 0.8 copy-start.8
  101.7 11.0 %collective-permute-start.3 = (bf16[1,2,512,128]{3,2,1,0:T(8,128)(2,1)S(1)}, bf16[1,2,512,128]{3,2,1,0:T(8,128)(2,1)S(1)}, u32[]{:S(2)}, u32[]{:S(2)}) collective-permute-start(bf16[1,2,512,128]{3,2,1,0:T(8,128)(2,1)S(1)} %maximum_bitcast_fusion.2), channel_id=1, source_target_pairs={{4,0},{8,4},{12,8},{16,12},{20,16},{24,20},{28,24},{32,28},{36,32}... | collective-permute-start | bytes 786440 | tf_op jit(solution)/shard_map/ppermute | solution.py:21
  112.7 25.6 %copy-start.1 = (bf16[1,512,1024]{2,1,0:T(8,128)(2,1)S(1)}, bf16[1,512,1024]{2,1,0:T(8,128)(2,1)}, u32[]{:S(2)}) copy-start(bf16[1,512,1024]{2,1,0:T(8,128)(2,1)} %stack_reshape.7) | copy-start | bytes 3145732
  115.9 10.1 %all-to-all-start.3 = ((bf16[1,2,512,128]{3,1,0,2:T(2,128)(2,1)}), bf16[1,2,512,128]{3,1,0,2:T(2,128)(2,1)S(1)}, u32[]{:S(2)}, u32[]{:S(2)}) async-start(bf16[1,2,512,128]{3,1,0,2:T(2,128)(2,1)} %copy.71), calls=%async_computation.3 | async-start | bytes 524288 | tf_op jit(solution)/shard_map/all_to_all | solution.py:165
  126.0 16.1 %all-to-all-start.2 = ((bf16[1,2,512,128]{3,1,0,2:T(2,128)(2,1)}), bf16[1,2,512,128]{3,1,0,2:T(2,128)(2,1)S(1)}, u32[]{:S(2)}, u32[]{:S(2)}) async-start(bf16[1,2,512,128]{3,1,0,2:T(2,128)(2,1)} %maximum_bitcast_fusion.3), calls=%async_computation.2 | async-start | bytes 524288 | tf_op jit(solution)/shard_map/all_to_all | solution.py:164
where the time goes:
time: 144 us; the launch traced here: 143 us
  local copies, waits for them, and re-layouts  39.7 us (28%)
  matrix products  36.2 us (25%)
  starting transfers between devices  34.9 us (24%)
  other arithmetic  24.1 us (17%)
  waiting for transfers between devices  6.8 us (5%)
    unnamed x57, local copies, waits for them, and re-layouts  19.9 us
    ppermute x2, starting transfers between devices, padded_2(): lax.ppermute(head, axis, [((i + 1) % count, i) for i in range(ends)])  11.4 us
    dot_general x2, matrix products, span_grads(): jnp.einsum('btgjd,bkgd->bgjtk', do_blocks, v_windows, preferred_element_t...  8.42 us
    dot_general x2, matrix products, span_grads(): jnp.einsum('bgjtk,bkgd->btgjd', probs_b, v_windows, preferred_element_typ...  7.54 us
    dot_general x2, matrix products, span_grads(): jnp.einsum('bgjtk,btgjd->bkgd', probs_b, do_blocks, preferred_element_typ...  7.32 us
    dot_general x2, matrix products, span_grads(): jnp.einsum('bgjtk,bkgd->btgjd', dscores, k_windows, preferred_element_typ...  6.55 us
    convert_element_type x2, local copies, waits for them, and re-layouts, span_grads(): do_blocks.astype(jnp.float32) * outputs.astype(jnp.float32)  5.78 us
    all_to_all x1, starting transfers between devices, per_device(): lax.all_to_all(value_layout, 'head', split_axis=2, concat_axis=3, tiled=T...  4.84 us
  transfers between devices with their start and end apart: 8, of which 2 were waited for; matrix products, arithmetic and copies ran while one was open for 60% of the time, Pallas kernels for 0%

commit v1 on v0

--- a/solution.py
+++ b/solution.py
@@ -6,6 +6,12 @@
 HD = 128
 BLK = 128
 GROUP = 8
+
+
+def exchange_blocks(array, axis, split, join):
+    cells = jnp.split(array, lax.axis_size(axis), axis=split)
+    received = lax.all_to_all(jnp.stack(cells), axis, 0, 0)
+    return jnp.concatenate(received, axis=join)
 
 
 def padded_2(cells, sides, width):
@@ -97,7 +103,7 @@
 
 def per_device(query, key, value, d_out, doc_start):
     kv_key, kv_value = (
-        lax.all_to_all(key, "head", split_axis=3, concat_axis=2, tiled=True),
+        exchange_blocks(key, "head", 3, 2),
         lax.all_to_all(value, "head", split_axis=3, concat_axis=2, tiled=True),
     )
     span_rows = kv_key.shape[2]

time: 144 us -> 134 us (0.931)
  other arithmetic: 24.1 us -> 18.5 us
  local copies, waits for them, and re-layouts: 39.7 us -> 34.3 us
    all_to_all x1, waiting for transfers between devices: 4.33 us -> 0.01 us  [per_device(): lax.all_to_all(value, 'head', split_axis=3, concat_axis=2, tiled=True)]
    all_to_all x1, waiting for transfers between devices: 0.01 us -> 4.33 us  [exchange_blocks(): received = lax.all_to_all(jnp.stack(cells), axis, 0, 0)]
    ppermute x2, waiting for transfers between devices: 0.01 us -> 3.86 us  [padded_2(): lax.ppermute(head, axis, [((i + 1) % count, i) for i in range(ends)])]
    unnamed x57 -> x52, local copies, waits for them, and re-layouts: 19.9 us -> 16.3 us
    dot_general x2, matrix products: 6.55 us -> 9.01 us  [span_grads(): jnp.einsum('bgjtk,bkgd->btgjd', dscores, k_windows, preferred_element_typ...]
    all_to_all x1, waiting for transfers between devices: 2.45 us -> 0.01 us  [per_device(): lax.all_to_all(value_layout, 'head', split_axis=2, concat_axis=3, tiled=T...]
    convert_element_type x2, other arithmetic: 2.15 us -> 0.16 us  [per_device(): value_grads.append(own_value.astype(jnp.bfloat16))]
  transfers between devices with their start and end apart: 8 -> 8, of which waited for: 2 -> 2; matrix products, arithmetic and copies ran while one was open for 60% -> 61% of each run, Pallas kernels for 0% -> 0%
where the time goes in v1:
time: 134 us; the launch traced here: 133 us
  matrix products  36.4 us (27%)
  starting transfers between devices  34.6 us (26%)
  local copies, waits for them, and re-layouts  34.3 us (26%)
  other arithmetic  18.5 us (14%)
  waiting for transfers between devices  8.2 us (6%)
  between operations  1.38 us (1%)
    unnamed x52, local copies, waits for them, and re-layouts  16.3 us
    ppermute x2, starting transfers between devices, padded_2(): lax.ppermute(head, axis, [((i + 1) % count, i) for i in range(ends)])  11.1 us
    dot_general x2, matrix products, span_grads(): jnp.einsum('bgjtk,bkgd->btgjd', dscores, k_windows, preferred_element_typ...  9.01 us
    dot_general x2, matrix products, span_grads(): jnp.einsum('btgjd,bkgd->bgjtk', do_blocks, v_windows, preferred_element_t...  8.43 us
    dot_general x2, matrix products, span_grads(): jnp.einsum('bgjtk,bkgd->btgjd', probs_b, v_windows, preferred_element_typ...  6.34 us
    dot_general x2, matrix products, span_grads(): jnp.einsum('bgjtk,btgjd->bkgd', probs_b, do_blocks, preferred_element_typ...  6.25 us
    convert_element_type x2, local copies, waits for them, and re-layouts, span_grads(): do_blocks.astype(jnp.float32) * outputs.astype(jnp.float32)  5.85 us
    reduce_sum x2, other arithmetic, span_grads(): probs = weights / jnp.sum(weights, axis=-1, keepdims=True)  4.89 us
  transfers between devices with their start and end apart: 8, of which 2 were waited for; matrix products, arithmetic and copies ran while one was open for 61% of the time, Pallas kernels for 0%

profile of v1, /device:TPU:26, one launch (start us, length us, event | category | flops | bytes accessed | tf_op | source)
XLA Modules:
  0.0 133.4 jit_solution(2179701548588943336)
XLA Ops:
  0.6 1.8 %copy.43 = bf16[1,2,128,512]{2,1,0,3:T(2,128)(2,1)} copy(bf16[1,2,128,512]{3,2,1,0:T(8,128)(2,1)} %param.23) | data formatting | bytes 524288 | tf_op args[2]
  2.5 4.8 %all-to-all-start.1 = ((bf16[1,2,128,512]{2,1,0,3:T(2,128)(2,1)}), bf16[1,2,128,512]{2,1,0,3:T(2,128)(2,1)S(1)}, u32[]{:S(2)}, u32[]{:S(2)}) async-start(bf16[1,2,128,512]{2,1,0,3:T(2,128)(2,1)} %copy.43), calls=%async_computation.1 | async-start | bytes 524288 | tf_op jit(solution)/shard_map/all_to_all | solution.py:107
  9.5 1.7 %slice_bitcast_fusion.1 = (bf16[64,8,8,128]{3,1,2,0:T(8,128)(2,1)S(1)}, bf16[64,8,8,128]{3,1,2,0:T(8,128)(2,1)S(1)}) fusion(bf16[1,2,512,1024]{3,2,1,0:T(8,128)(2,1)} %param.21), kind=kLoop, calls=%fused_computation.56 | loop fusion | bytes 4194304
  11.3 4.7 %slice_bitcast_fusion.3 = (bf16[64,8,8,128]{3,1,2,0:T(8,128)(2,1)}, f32[64,8,8,128]{3,1,2,0:T(8,128)}, f32[64,8,8,128]{3,1,2,0:T(8,128)}, bf16[64,8,8,128]{3,1,2,0:T(8,128)(2,1)}) fusion(bf16[1,2,512,1024]{3,2,1,0:T(8,128)(2,1)} %param.24), kind=kLoop, calls=%fused_computation.68 | loop fusion | flops 1048576 | bytes 8388608
  16.8 4.8 %all-to-all-start = ((bf16[4,1,2,128,128]{4,3,2,1,0:T(8,128)(2,1)}), bf16[4,1,2,128,128]{4,3,2,1,0:T(8,128)(2,1)S(1)}, u32[]{:S(2)}, u32[]{:S(2)}) async-start(bf16[4,1,2,128,128]{4,3,2,1,0:T(8,128)(2,1)} %pad_maximum_fusion.1), calls=%async_computation | async-start | bytes 524288 | tf_op jit(solution)/shard_map/all_to_all | solution.py:13
  22.5 4.3 %all-to-all-done = bf16[4,1,2,128,128]{4,3,2,1,0:T(8,128)(2,1)S(1)} async-done(((bf16[4,1,2,128,128]{4,3,2,1,0:T(8,128)(2,1)}), bf16[4,1,2,128,128]{4,3,2,1,0:T(8,128)(2,1)S(1)}, u32[]{:S(2)}, u32[]{:S(2)}) %all-to-all-start) | async-done | bytes 262176 | tf_op jit(solution)/shard_map/all_to_all | solution.py:13
  28.5 5.4 %collective-permute-start.1 = (bf16[1,2,512,128]{3,2,1,0:T(8,128)(2,1)}, bf16[1,2,512,128]{3,2,1,0:T(8,128)(2,1)}, u32[]{:S(2)}, u32[]{:S(2)}) collective-permute-start(bf16[1,2,512,128]{3,2,1,0:T(8,128)(2,1)} %maximum_bitcast_fusion.1), channel_id=1, source_target_pairs={{4,0},{8,4},{12,8},{16,12},{20,16},{24,20},{28,24},{32,28},{36,32}... | collective-permute-start | bytes 786440 | tf_op jit(solution)/shard_map/ppermute | solution.py:27
  34.6 2.6 %copy.94 = bf16[64,8,8,128]{3,2,1,0:T(8,128)(2,1)} copy(bf16[64,8,8,128]{3,1,2,0:T(8,128)(2,1)} %get-tuple-element.83) | data formatting | bytes 2097152
  37.2 2.5 %copy.97 = bf16[64,8,8,128]{3,2,1,0:T(8,128)(2,1)} copy(bf16[64,8,8,128]{3,1,2,0:T(8,128)(2,1)} %get-tuple-element.86) | data formatting | bytes 2097152
  39.7 3.4 %copy.95 = f32[64,8,8,128]{3,2,1,0:T(8,128)} copy(f32[64,8,8,128]{3,1,2,0:T(8,128)} %get-tuple-element.84) | data formatting | bytes 4194304
  43.1 3.0 %copy.49 = f32[4,128,1,8,128]{1,4,3,0,2:T(8,128)} copy(f32[4,128,1,8,128]{4,3,2,1,0:T(8,128)} %bitcast.427) | data formatting | bytes 4194304 | tf_op jit(solution)/shard_map/convert_element_type | solution.py:81
  46.1 3.4 %copy.98 = f32[64,8,8,128]{3,2,1,0:T(8,128)} copy(f32[64,8,8,128]{3,1,2,0:T(8,128)} %get-tuple-element.85) | data formatting | bytes 4194304
  49.4 2.9 %copy.57 = f32[4,128,1,8,128]{1,4,3,0,2:T(8,128)} copy(f32[4,128,1,8,128]{4,3,2,1,0:T(8,128)} %bitcast.428) | data formatting | bytes 4194304 | tf_op jit(solution)/shard_map/convert_element_type | solution.py:81
  54.4 2.1 %collective-permute-start = (bf16[1,2,512,128]{3,2,1,0:T(8,128)(2,1)S(1)}, bf16[1,2,512,128]{3,2,1,0:T(8,128)(2,1)S(1)}, u32[]{:S(2)}, u32[]{:S(2)}) collective-permute-start(bf16[1,2,512,128]{3,2,1,0:T(8,128)(2,1)S(1)} %get-tuple-element.135), channel_id=1, source_target_pairs={{0,4},{4,8},{8,12},{12,16},{16,20},{20,24},{24,28},{28,32},{32,36}... | collective-permute-start | bytes 786440 | tf_op jit(solution)/shard_map/ppermute | solution.py:25
  58.6 2.4 %fusion.15 = f32[4,8,128]{2,1,0:T(8,128)S(1)} fusion(f32[4,640,128,8]{2,1,3,0:T(8,128)S(1)} %get-tuple-element.156, f32[4,8,128]{2,1,0:T(8,128)S(1)} %get-tuple-element.155, pred[4,128,640]{1,2,0:T(8,128)(4,1)S(1)} %get-tuple-element.152), kind=kLoop, calls=%fused_computation.21 | loop fusion | flops 10481664 | bytes 10846208 | tf_op jit(solution)/shard_map/reduce_sum | solution.py:76
  61.1 3.1 %fusion.41 = f32[4,640,1,128]{3,1,0,2:T(8,128)S(1)} fusion(bf16[4,128,8,128]{3,2,1,0:T(8,128)(2,1)S(1)} %bitcast.451, f32[4,8,128]{2,1,0:T(8,128)S(1)} %fusion.15, f32[4,8,128]{2,1,0:T(8,128)S(1)} %get-tuple-element.155, f32[4,640,128,8]{2,1,3,0:T(8,128)S(1)} %get-tuple-element.156, pred[4,128,640]{1,2,0:T(8,128)(4,1)S(1)} %get-tuple-element.152), kind=kOutput, calls=%fused_computation.50 | convolution fusion | flops 684195840 | bytes 13205504 | tf_op jit(solution)/shard_map/bgjtk,btgjd->bkgd/dot_general | solution.py:94
  64.2 3.2 %fusion.29 = f32[4,128,8]{1,2,0:T(8,128)S(1)} fusion(f32[4,128,1,8,128]{1,4,3,0,2:T(8,128)S(1)} %copy-done.3, bf16[4,640,1,128]{3,1,0,2:T(8,128)(2,1)S(1)} %constant_dynamic-update-slice_fusion.15, f32[4,8,128]{2,1,0:T(8,128)S(1)} %fusion.15, f32[4,8,128]{2,1,0:T(8,128)S(1)} %get-tuple-element.155, f32[4,640,128,8]{2,1,3,0:T(8,128)S(1)} %get-tuple-element.156, ...), kind=kOutput, calls=%fused_computation.37 | convolution fusion | flops 686288896 | bytes 13615104 | tf_op jit(solution)/shard_map/bgjtk,bkgd->btgjd/dot_general | solution.py:78
  67.4 4.2 %fusion.17 = bf16[4,8,128,640]{2,3,1,0:T(8,128)(2,1)S(1)} fusion(f32[4,8,128]{2,1,0:T(8,128)S(1)} %bitcast.478, f32[4,8,128]{2,1,0:T(8,128)S(1)} %fusion.15, f32[4,8,128]{2,1,0:T(8,128)S(1)} %get-tuple-element.155, f32[4,640,128,8]{2,1,3,0:T(8,128)S(1)} %get-tuple-element.156, pred[4,128,640]{1,2,0:T(8,128)(4,1)S(1)} %get-tuple-element.152, ...), kind=kOutput, calls=%fused_computation.23 | convolution fusion | flops 692060160 | bytes 17809408 | tf_op jit(solution)/shard_map/btgjd,bkgd->bgjtk/dot_general | solution.py:82
  73.6 2.1 %collective-permute-start.2 = (bf16[1,2,512,128]{3,2,1,0:T(8,128)(2,1)S(1)}, bf16[1,2,512,128]{3,2,1,0:T(8,128)(2,1)S(1)}, u32[]{:S(2)}, u32[]{:S(2)}) collective-permute-start(bf16[1,2,512,128]{3,2,1,0:T(8,128)(2,1)S(1)} %fusion.76), channel_id=1, source_target_pairs={{0,4},{4,8},{8,12},{12,16},{16,20},{20,24},{24,28},{28,32},{32,36}... | collective-permute-start | bytes 786440 | tf_op jit(solution)/shard_map/ppermute | solution.py:25
  78.0 2.4 %fusion.13 = f32[4,8,128]{2,1,0:T(8,128)S(1)} fusion(f32[4,640,128,8]{2,1,3,0:T(8,128)S(1)} %get-tuple-element.158, f32[4,8,128]{2,1,0:T(8,128)S(1)} %get-tuple-element.157, pred[4,128,640]{1,2,0:T(8,128)(4,1)S(1)} %get-tuple-element.151), kind=kLoop, calls=%fused_computation.19 | loop fusion | flops 10481664 | bytes 10846208 | tf_op jit(solution)/shard_map/reduce_sum | solution.py:76
  80.4 3.1 %fusion.38 = f32[4,640,1,128]{3,1,0,2:T(8,128)S(1)} fusion(bf16[4,128,8,128]{3,2,1,0:T(8,128)(2,1)S(1)} %bitcast.449, f32[4,8,128]{2,1,0:T(8,128)S(1)} %fusion.13, f32[4,8,128]{2,1,0:T(8,128)S(1)} %get-tuple-element.157, f32[4,640,128,8]{2,1,3,0:T(8,128)S(1)} %get-tuple-element.158, pred[4,128,640]{1,2,0:T(8,128)(4,1)S(1)} %get-tuple-element.151), kind=kOutput, calls=%fused_computation.49 | convolution fusion | flops 684195840 | bytes 13205504 | tf_op jit(solution)/shard_map/bgjtk,btgjd->bkgd/dot_general | solution.py:94
  83.6 3.2 %fusion.31 = f32[4,128,8]{1,2,0:T(8,128)S(1)} fusion(f32[4,128,1,8,128]{1,4,3,0,2:T(8,128)S(1)} %copy-done.2, bf16[4,640,1,128]{3,1,0,2:T(8,128)(2,1)S(1)} %constant_dynamic-update-slice_fusion.5, f32[4,8,128]{2,1,0:T(8,128)S(1)} %fusion.13, f32[4,8,128]{2,1,0:T(8,128)S(1)} %get-tuple-element.157, f32[4,640,128,8]{2,1,3,0:T(8,128)S(1)} %get-tuple-element.158, ...), kind=kOutput, calls=%fused_computation.40 | convolution fusion | flops 686288896 | bytes 13615104 | tf_op jit(solution)/shard_map/bgjtk,bkgd->btgjd/dot_general | solution.py:78
  86.7 4.2 %fusion.16 = bf16[4,8,128,640]{2,3,1,0:T(8,128)(2,1)S(1)} fusion(f32[4,8,128]{2,1,0:T(8,128)S(1)} %bitcast.479, f32[4,8,128]{2,1,0:T(8,128)S(1)} %fusion.13, f32[4,8,128]{2,1,0:T(8,128)S(1)} %get-tuple-element.157, f32[4,640,128,8]{2,1,3,0:T(8,128)S(1)} %get-tuple-element.158, pred[4,128,640]{1,2,0:T(8,128)(4,1)S(1)} %get-tuple-element.151, ...), kind=kOutput, calls=%fused_computation.22 | convolution fusion | flops 692060160 | bytes 17809408 | tf_op jit(solution)/shard_map/btgjd,bkgd->bgjtk/dot_general | solution.py:82
  93.0 5.8 %collective-permute-start.3 = (bf16[1,2,512,128]{3,2,1,0:T(8,128)(2,1)S(1)}, bf16[1,2,512,128]{3,2,1,0:T(8,128)(2,1)S(1)}, u32[]{:S(2)}, u32[]{:S(2)}) collective-permute-start(bf16[1,2,512,128]{3,2,1,0:T(8,128)(2,1)S(1)} %maximum_bitcast_fusion.2), channel_id=1, source_target_pairs={{4,0},{8,4},{12,8},{16,12},{20,16},{24,20},{28,24},{32,28},{36,32}... | collective-permute-start | bytes 786440 | tf_op jit(solution)/shard_map/ppermute | solution.py:27
  98.7 3.9 %collective-permute-done.3 = bf16[1,2,512,128]{3,2,1,0:T(8,128)(2,1)S(1)} collective-permute-done((bf16[1,2,512,128]{3,2,1,0:T(8,128)(2,1)S(1)}, bf16[1,2,512,128]{3,2,1,0:T(8,128)(2,1)S(1)}, u32[]{:S(2)}, u32[]{:S(2)}) %collective-permute-start.3) | collective-permute-done | bytes 262176 | tf_op jit(solution)/shard_map/ppermute | solution.py:27
  103.9 4.8 %all-to-all-start.3 = ((bf16[1,2,512,128]{3,1,0,2:T(2,128)(2,1)}), bf16[1,2,512,128]{3,1,0,2:T(2,128)(2,1)S(1)}, u32[]{:S(2)}, u32[]{:S(2)}) async-start(bf16[1,2,512,128]{3,1,0,2:T(2,128)(2,1)} %copy.67), calls=%async_computation.3 | async-start | bytes 524288 | tf_op jit(solution)/shard_map/all_to_all | solution.py:171
  108.7 4.5 %fusion.45 = bf16[4,128,1,8,128]{1,4,3,0,2:T(8,128)(2,1)} fusion(bf16[4,8,128,640]{2,3,1,0:T(8,128)(2,1)} %copy-done, bf16[4,640,1,128]{3,1,0,2:T(8,128)(2,1)S(1)} %constant_dynamic-update-slice_fusion.10), kind=kOutput, calls=%fused_computation.52 | convolution fusion | flops 671612928 | bytes 6946816 | tf_op jit(solution)/shard_map/bgjtk,bkgd->btgjd/dot_general | solution.py:88
  113.2 1.7 %copy.60 = bf16[4,128,1,8,128]{4,3,1,0,2:T(8,128)(2,1)S(1)} copy(bf16[4,128,1,8,128]{1,4,3,0,2:T(8,128)(2,1)} %fusion.45) | data formatting | bytes 2097152 | tf_op jit(solution)/shard_map/convert_element_type | solution.py:90
  116.4 4.8 %all-to-all-start.2 = ((bf16[1,2,512,128]{3,1,0,2:T(2,128)(2,1)}), bf16[1,2,512,128]{3,1,0,2:T(2,128)(2,1)S(1)}, u32[]{:S(2)}, u32[]{:S(2)}) async-start(bf16[1,2,512,128]{3,1,0,2:T(2,128)(2,1)} %copy.65), calls=%async_computation.2 | async-start | bytes 524288 | tf_op jit(solution)/shard_map/all_to_all | solution.py:170
  121.2 4.5 %fusion.44 = bf16[4,128,1,8,128]{1,4,3,0,2:T(8,128)(2,1)} fusion(bf16[4,8,128,640]{2,3,1,0:T(8,128)(2,1)} %copy-done.1, bf16[4,640,1,128]{3,1,0,2:T(8,128)(2,1)S(1)} %constant_dynamic-update-slice_fusion), kind=kOutput, calls=%fused_computation.51 | convolution fusion | flops 671612928 | bytes 6946816 | tf_op jit(solution)/shard_map/bgjtk,bkgd->btgjd/dot_general | solution.py:88
  125.7 1.7 %copy.52 = bf16[4,128,1,8,128]{4,3,1,0,2:T(8,128)(2,1)S(1)} copy(bf16[4,128,1,8,128]{1,4,3,0,2:T(8,128)(2,1)} %fusion.44) | data formatting | bytes 2097152 | tf_op jit(solution)/shard_map/convert_element_type | solution.py:90
  128.6 2.7 %maximum_bitcast_fusion = bf16[1,2,512,1024]{3,2,1,0:T(8,128)(2,1)} fusion(bf16[1,512,1024]{2,1,0:T(8,128)(2,1)S(1)} %stack_reshape.7, bf16[1,512,1024]{2,1,0:T(8,128)(2,1)} %stack_reshape.6), kind=kLoop, calls=%fused_computation.34 | loop fusion | flops 1048576 | bytes 4194304 | tf_op jit(solution)/shard_map/broadcast_in_dim | solution.py:166
  (113 shorter events, 22.3 us)
Async XLA Ops:
  2.5 14.3 %all-to-all-start.1 = ((bf16[1,2,128,512]{2,1,0,3:T(2,128)(2,1)}), bf16[1,2,128,512]{2,1,0,3:T(2,128)(2,1)S(1)}, u32[]{:S(2)}, u32[]{:S(2)}) async-start(bf16[1,2,128,512]{2,1,0,3:T(2,128)(2,1)} %copy.43), calls=%async_computation.1 | async-start | bytes 524288 | tf_op jit(solution)/shard_map/all_to_all | solution.py:107
  16.8 10.0 %all-to-all-start = ((bf16[4,1,2,128,128]{4,3,2,1,0:T(8,128)(2,1)}), bf16[4,1,2,128,128]{4,3,2,1,0:T(8,128)(2,1)S(1)}, u32[]{:S(2)}, u32[]{:S(2)}) async-start(bf16[4,1,2,128,128]{4,3,2,1,0:T(8,128)(2,1)} %pad_maximum_fusion.1), calls=%async_computation | async-start | bytes 524288 | tf_op jit(solution)/shard_map/all_to_all | solution.py:13
  28.5 24.8 %collective-permute-start.1 = (bf16[1,2,512,128]{3,2,1,0:T(8,128)(2,1)}, bf16[1,2,512,128]{3,2,1,0:T(8,128)(2,1)}, u32[]{:S(2)}, u32[]{:S(2)}) collective-permute-start(bf16[1,2,512,128]{3,2,1,0:T(8,128)(2,1)} %maximum_bitcast_fusion.1), channel_id=1, source_target_pairs={{4,0},{8,4},{12,8},{16,12},{20,16},{24,20},{28,24},{32,28},{36,32}... | collective-permute-start | bytes 786440 | tf_op jit(solution)/shard_map/ppermute | solution.py:27
  34.5 17.8 %copy-start.13 = (pred[128,640]{0,1:T(8,128)(4,1)S(1)}, pred[128,640]{0,1:T(8,128)(4,1)}, u32[]{:S(2)}) copy-start(pred[128,640]{0,1:T(8,128)(4,1)} %iota_compare_fusion) | copy-start | bytes 245764
  34.6 18.8 %copy-start.11 = (bf16[1,512,128]{2,1,0:T(8,128)(2,1)S(1)}, bf16[1,512,128]{2,1,0:T(8,128)(2,1)}, u32[]{:S(2)}) copy-start(bf16[1,512,128]{2,1,0:T(8,128)(2,1)} %get-tuple-element.114) | copy-start | bytes 393220
  34.6 18.8 %copy-start.12 = (bf16[1,512,128]{2,1,0:T(8,128)(2,1)S(1)}, bf16[1,512,128]{2,1,0:T(8,128)(2,1)}, u32[]{:S(2)}) copy-start(bf16[1,512,128]{2,1,0:T(8,128)(2,1)} %get-tuple-element.163) | copy-start | bytes 393220
  37.2 19.4 %copy-start.6 = (bf16[512,128]{1,0:T(8,128)(2,1)S(1)}, bf16[512,128]{1,0:T(8,128)(2,1)}, u32[]{:S(2)}) copy-start(bf16[512,128]{1,0:T(8,128)(2,1)} %get-tuple-element.117) | copy-start | bytes 393220
  39.7 17.1 %copy-start.10 = (bf16[1,1,512,128]{3,2,1,0:T(8,128)(2,1)S(1)}, bf16[1,1,512,128]{3,2,1,0:T(8,128)(2,1)}, u32[]{:S(2)}) copy-start(bf16[1,1,512,128]{3,2,1,0:T(8,128)(2,1)} %get-tuple-element.159) | copy-start | bytes 393220
  43.1 13.8 %copy-start.9 = (bf16[1,1,512,128]{3,2,1,0:T(8,128)(2,1)S(1)}, bf16[1,1,512,128]{3,2,1,0:T(8,128)(2,1)}, u32[]{:S(2)}) copy-start(bf16[1,1,512,128]{3,2,1,0:T(8,128)(2,1)} %get-tuple-element.118) | copy-start | bytes 393220
  54.4 21.4 %collective-permute-start = (bf16[1,2,512,128]{3,2,1,0:T(8,128)(2,1)S(1)}, bf16[1,2,512,128]{3,2,1,0:T(8,128)(2,1)S(1)}, u32[]{:S(2)}, u32[]{:S(2)}) collective-permute-start(bf16[1,2,512,128]{3,2,1,0:T(8,128)(2,1)S(1)} %get-tuple-element.135), channel_id=1, source_target_pairs={{0,4},{4,8},{8,12},{12,16},{16,20},{20,24},{24,28},{28,32},{32,36}... | collective-permute-start | bytes 786440 | tf_op jit(solution)/shard_map/ppermute | solution.py:25
  56.9 4.1 %copy-start.5 = (bf16[64,8,8,128]{3,2,1,0:T(8,128)(2,1)S(1)}, bf16[64,8,8,128]{3,2,1,0:T(8,128)(2,1)}, u32[]{:S(2)}) copy-start(bf16[64,8,8,128]{3,2,1,0:T(8,128)(2,1)} %copy.97) | copy-start | bytes 3145732
  61.1 3.1 %copy-start.3 = (f32[4,128,1,8,128]{1,4,3,0,2:T(8,128)S(1)}, f32[4,128,1,8,128]{1,4,3,0,2:T(8,128)}, u32[]{:S(2)}) copy-start(f32[4,128,1,8,128]{1,4,3,0,2:T(8,128)} %copy.57) | copy-start | bytes 6291460
  71.6 4.4 %copy-start = (bf16[4,8,128,640]{2,3,1,0:T(8,128)(2,1)}, bf16[4,8,128,640]{2,3,1,0:T(8,128)(2,1)S(1)}, u32[]{:S(2)}) copy-start(bf16[4,8,128,640]{2,3,1,0:T(8,128)(2,1)S(1)} %fusion.17) | copy-start | bytes 15728644
  71.6 4.5 %copy-start.8 = (bf16[1,1,512,128]{3,2,1,0:T(8,128)(2,1)S(1)}, bf16[1,1,512,128]{3,2,1,0:T(8,128)(2,1)}, u32[]{:S(2)}) copy-start(bf16[1,1,512,128]{3,2,1,0:T(8,128)(2,1)} %get-tuple-element.164) | copy-start | bytes 393220
  71.7 4.5 %copy-start.7 = (bf16[1,1,512,128]{3,2,1,0:T(8,128)(2,1)S(1)}, bf16[1,1,512,128]{3,2,1,0:T(8,128)(2,1)}, u32[]{:S(2)}) copy-start(bf16[1,1,512,128]{3,2,1,0:T(8,128)(2,1)} %get-tuple-element.113) | copy-start | bytes 393220
  73.6 25.1 %collective-permute-start.2 = (bf16[1,2,512,128]{3,2,1,0:T(8,128)(2,1)S(1)}, bf16[1,2,512,128]{3,2,1,0:T(8,128)(2,1)S(1)}, u32[]{:S(2)}, u32[]{:S(2)}) collective-permute-start(bf16[1,2,512,128]{3,2,1,0:T(8,128)(2,1)S(1)} %fusion.76), channel_id=1, source_target_pairs={{0,4},{4,8},{8,12},{12,16},{16,20},{20,24},{24,28},{28,32},{32,36}... | collective-permute-start | bytes 786440 | tf_op jit(solution)/shard_map/ppermute | solution.py:25
  76.3 4.1 %copy-start.4 = (bf16[64,8,8,128]{3,2,1,0:T(8,128)(2,1)S(1)}, bf16[64,8,8,128]{3,2,1,0:T(8,128)(2,1)}, u32[]{:S(2)}) copy-start(bf16[64,8,8,128]{3,2,1,0:T(8,128)(2,1)} %copy.94) | copy-start | bytes 3145732
  80.4 3.1 %copy-start.2 = (f32[4,128,1,8,128]{1,4,3,0,2:T(8,128)S(1)}, f32[4,128,1,8,128]{1,4,3,0,2:T(8,128)}, u32[]{:S(2)}) copy-start(f32[4,128,1,8,128]{1,4,3,0,2:T(8,128)} %copy.49) | copy-start | bytes 6291460
  91.0 11.8 %copy-start.1 = (bf16[4,8,128,640]{2,3,1,0:T(8,128)(2,1)}, bf16[4,8,128,640]{2,3,1,0:T(8,128)(2,1)S(1)}, u32[]{:S(2)}) copy-start(bf16[4,8,128,640]{2,3,1,0:T(8,128)(2,1)S(1)} %fusion.16) | copy-start | bytes 15728644
  93.0 9.6 %collective-permute-start.3 = (bf16[1,2,512,128]{3,2,1,0:T(8,128)(2,1)S(1)}, bf16[1,2,512,128]{3,2,1,0:T(8,128)(2,1)S(1)}, u32[]{:S(2)}, u32[]{:S(2)}) collective-permute-start(bf16[1,2,512,128]{3,2,1,0:T(8,128)(2,1)S(1)} %maximum_bitcast_fusion.2), channel_id=1, source_target_pairs={{4,0},{8,4},{12,8},{16,12},{20,16},{24,20},{28,24},{32,28},{36,32}... | collective-permute-start | bytes 786440 | tf_op jit(solution)/shard_map/ppermute | solution.py:27
  103.9 12.5 %all-to-all-start.3 = ((bf16[1,2,512,128]{3,1,0,2:T(2,128)(2,1)}), bf16[1,2,512,128]{3,1,0,2:T(2,128)(2,1)S(1)}, u32[]{:S(2)}, u32[]{:S(2)}) async-start(bf16[1,2,512,128]{3,1,0,2:T(2,128)(2,1)} %copy.67), calls=%async_computation.3 | async-start | bytes 524288 | tf_op jit(solution)/shard_map/all_to_all | solution.py:171
  116.4 16.0 %all-to-all-start.2 = ((bf16[1,2,512,128]{3,1,0,2:T(2,128)(2,1)}), bf16[1,2,512,128]{3,1,0,2:T(2,128)(2,1)S(1)}, u32[]{:S(2)}, u32[]{:S(2)}) async-start(bf16[1,2,512,128]{3,1,0,2:T(2,128)(2,1)} %copy.65), calls=%async_computation.2 | async-start | bytes 524288 | tf_op jit(solution)/shard_map/all_to_all | solution.py:170
